TPU v7x, 256 devices: a whole 4x4x8 slice. The times are simulated.
256 devices in a mesh: tm: 64 (over y_hi, z, x), head: 4 (over y_lo, core).
Axes of the slice: x: 4, y: 4 (y_hi: 2, y_lo: 2; y = y_hi * 2 + y_lo), z: 8, core: 2. Of those that a mesh axis runs over, the one named last changes fastest.
Arguments:
- frames: bfloat16 [64, 512, 1152], P('tm', None, 'head'), may hold values from -6 to 6
- modulation: float32 [3, 1152], replicated, may hold values from -4 to 4
- w_qkv: bfloat16 [3, 1152, 1152], P(None, None, 'head'), may hold values from -1 to 1
- w_out: bfloat16 [1152, 1152], P('head'), may hold values from -0.375 to 0.375
- conv_taps: float32 [3, 1152], P(None, 'head'), may hold values from -3 to 3
- anchors: int32 [4], replicated, may hold values from 0 to 15
Outputs:
- block_out: bfloat16 [64, 512, 1152], P('tm', None, 'head')
All inputs are finite; a program needn't handle non-finite values.
Results may differ from a plain program's by a relative error of at most 0.011.
Values may be sent and summed in bfloat16 or wider, within the bound.
A program may use at most 64 MiB of HBM per device.

v0:
```python
import jax
import jax.numpy as jnp
from jax import lax
from jax.sharding import PartitionSpec as P

HS = 72
SEG = 16
EPSILON = 1e-06


def swapped(block, axis, stride):
    count = lax.axis_size(axis)
    route = []
    for low in range(count):
        high = low | 1 << stride
        if high != low and high < count:
            route += [(low, high), (high, low)]
    return lax.ppermute(block, axis, route)


def extended(x, sides, width):
    for axis, dim in sides:
        size, length = (lax.axis_size(axis), x.shape[dim])
        up = [(i, (i + 1) % size) for i in range(size - 1)]
        down = [(j, i) for i, j in up]
        last = lax.slice_in_dim(x, length - width, length, axis=dim)
        leading = lax.slice_in_dim(x, 0, width, axis=dim)
        before = lax.ppermute(last, axis, up)
        after = lax.ppermute(leading, axis, down)
        x = jnp.concatenate([before, x, after], axis=dim)
    return x


def modulate(frame_rows, modulation):
    values = frame_rows.astype(jnp.float32)
    average = jnp.mean(values, axis=-1, keepdims=True)
    centred = values - average
    variance = jnp.mean(centred * centred, axis=-1, keepdims=True)
    normed = centred * lax.rsqrt(variance + EPSILON)
    return (normed * (1.0 + modulation[1]) + modulation[0]).astype(jnp.bfloat16)


def attend_block(queries, key_rows, value_rows):
    scores = jnp.einsum(
        "qhs,khs->hqk", queries, key_rows, preferred_element_type=jnp.float32
    ) * HS ** (-0.5)
    row_max = jnp.max(scores, axis=-1, keepdims=True)
    weights = jnp.exp(scores - row_max)
    weights = (weights / jnp.sum(weights, axis=-1, keepdims=True)).astype(jnp.bfloat16)
    return jnp.einsum(
        "hqk,khs->qhs", weights, value_rows, preferred_element_type=jnp.float32
    ).astype(jnp.bfloat16)


def local(frames, modulation, w_qkv, w_out, conv_taps, anchors):
    local_frames, tokens, width_dev = frames.shape
    group_size = SEG // local_frames
    tm_pos = lax.axis_index("tm")
    head_pos = lax.axis_index("head")
    gathered = lax.all_gather(frames, "head", axis=2, tiled=True)
    normed = modulate(gathered, modulation)
    projections = jnp.einsum(
        "fpd,cde->cfpe", normed, w_qkv, preferred_element_type=jnp.float32
    ).astype(jnp.bfloat16)
    segment = tm_pos * local_frames // SEG
    anchor_frame = segment * SEG + lax.dynamic_index_in_dim(anchors, segment, 0, keepdims=False)
    is_owner = anchor_frame // local_frames == tm_pos
    anchor_local = anchor_frame % local_frames
    own_part = lax.dynamic_index_in_dim(projections[1:], anchor_local, 1, keepdims=False)
    routed = jnp.where(is_owner, own_part, jnp.zeros_like(own_part))
    for bit_pos in range(group_size.bit_length() - 1):
        routed = routed + swapped(routed, "tm", bit_pos)
    heads_dev = width_dev // HS
    block_rows = min(512, tokens)
    anchor_keys = routed[0].reshape(tokens, heads_dev, HS)
    anchor_values = routed[1].reshape(tokens, heads_dev, HS)

    def frame_attention(pieces):
        queries, own_keys, own_values = pieces
        key_rows = jnp.concatenate([own_keys.reshape(tokens, heads_dev, HS), anchor_keys], axis=0)
        value_rows = jnp.concatenate(
            [own_values.reshape(tokens, heads_dev, HS), anchor_values], axis=0
        )
        query_blocks = queries.reshape(tokens // block_rows, block_rows, heads_dev, HS)

        def one_block(block_queries):
            return attend_block(block_queries, key_rows, value_rows)

        outputs = lax.map(one_block, query_blocks)
        return outputs.reshape(tokens, width_dev)

    attended = lax.map(frame_attention, (projections[0], projections[1], projections[2]))
    partial_terms = jnp.einsum("fpe,ed->fpd", attended, w_out, preferred_element_type=jnp.float32)
    summed = lax.psum_scatter(partial_terms, "head", scatter_dimension=2, tiled=True)
    gate_dev = lax.dynamic_slice_in_dim(modulation[2], head_pos * width_dev, width_dev)
    hidden = (frames.astype(jnp.float32) + gate_dev * summed).astype(jnp.bfloat16)
    padded = extended(hidden, (("tm", 0),), 1).astype(jnp.float32)
    block_out = (
        padded[1:-1]
        + conv_taps[0] * padded[:-2]
        + conv_taps[1] * padded[1:-1]
        + conv_taps[2] * padded[2:]
    )
    return block_out.astype(jnp.bfloat16)


def solution(mesh):
    in_specs = (
        P("tm", None, "head"),
        P(),
        P(None, None, "head"),
        P("head", None),
        P(None, "head"),
        P(),
    )
    out_specs = P("tm", None, "head")
    return jax.shard_map(local, mesh=mesh, in_specs=in_specs, out_specs=out_specs, check_vma=False)
```

profile of v0, /device:TPU:230, one launch (start us, length us, event | category | flops | bytes accessed | tf_op | source)
XLA Modules:
  0.0 228.0 jit_solution(18161637918810966751)
XLA Ops:
  7.3 1.2 dynamic_slice.21
  10.1 23.4 %all-gather.2.cloned.1.call-done = bf16[1,512,1152]{1,2,0:T(8,128)(2,1)} async-done(((bf16[1,512,288]{1,2,0:T(8,128)(2,1)}), bf16[1,512,1152]{1,2,0:T(8,128)(2,1)}) %all-gather.2.cloned.1.call-update) | async-done | bytes 1179664 | tf_op jit(solution)/shard_map/all_gather | solution.py:60
  33.5 1.6 convert_reduce_fusion
  35.1 1.6 fusion.8
  36.7 1.4 fusion.12
  38.2 0.9 collective-permute-start
  39.1 14.8 %collective-permute-done = bf16[2,512,288]{1,2,0:T(8,128)(2,1)S(1)} collective-permute-done((bf16[2,512,288]{1,2,0:T(8,128)(2,1)S(1)}, bf16[2,512,288]{1,2,0:T(8,128)(2,1)S(1)}, u32[]{:S(2)}, u32[]{:S(2)}) %collective-permute-start) | collective-permute-done | bytes 589856 | tf_op jit(solution)/shard_map/ppermute | solution.py:18
  54.0 1.5 collective-permute-start.1
  55.6 14.9 %collective-permute-done.1 = bf16[2,512,288]{1,2,0:T(8,128)(2,1)S(1)} collective-permute-done((bf16[2,512,288]{1,2,0:T(8,128)(2,1)S(1)}, bf16[2,512,288]{1,2,0:T(8,128)(2,1)S(1)}, u32[]{:S(2)}, u32[]{:S(2)}) %collective-permute-start.1) | collective-permute-done | bytes 589856 | tf_op jit(solution)/shard_map/ppermute | solution.py:18
  70.6 1.4 collective-permute-start.2
  72.0 12.6 %collective-permute-done.2 = bf16[2,512,288]{1,2,0:T(8,128)(2,1)S(1)} collective-permute-done((bf16[2,512,288]{1,2,0:T(8,128)(2,1)S(1)}, bf16[2,512,288]{1,2,0:T(8,128)(2,1)S(1)}, u32[]{:S(2)}, u32[]{:S(2)}) %collective-permute-start.2) | collective-permute-done | bytes 589856 | tf_op jit(solution)/shard_map/ppermute | solution.py:18
  84.8 2.3 collective-permute-start.3
  87.1 24.4 %collective-permute-done.3 = bf16[2,512,288]{1,2,0:T(8,128)(2,1)S(1)} collective-permute-done((bf16[2,512,288]{1,2,0:T(8,128)(2,1)S(1)}, bf16[2,512,288]{1,2,0:T(8,128)(2,1)S(1)}, u32[]{:S(2)}, u32[]{:S(2)}) %collective-permute-start.3) | collective-permute-done | bytes 589856 | tf_op jit(solution)/shard_map/ppermute | solution.py:18
  111.7 5.0 %fusion.41 = (f32[4,512]{1,0:T(4,128)S(1)}, f32[4,512,1024]{2,1,0:T(8,128)}) fusion(bf16[512,4,72]{0,2,1:T(8,128)(2,1)S(1)} %bitcast.35, bf16[512,4,72]{0,2,1:T(8,128)(2,1)S(1)} %bitcast.37, bf16[512,4,72]{0,2,1:T(8,128)(2,1)S(1)} %bitcast.34), kind=kOutput, calls=%fused_computation.57 | convolution fusion | flops 309462016 | bytes 9281536 | tf_op jit(solution)/shard_map/while/body/eval_jaxpr/while/body/eval_jaxpr/sub | solution.py:48
  116.7 4.9 %fusion.13 = bf16[4,72,512]{2,1,0:T(8,128)(2,1)S(1)} fusion(f32[4,512,1024]{2,1,0:T(8,128)} %get-tuple-element.58, f32[4,512]{1,0:T(4,128)S(1)} %get-tuple-element.57, bf16[512,4,72]{0,2,1:T(8,128)(2,1)S(1)} %bitcast.36, bf16[512,4,72]{0,2,1:T(8,128)(2,1)S(1)} %bitcast.33), kind=kOutput, calls=%fused_computation.18 | convolution fusion | flops 307511296 | bytes 9281536 | tf_op jit(solution)/shard_map/while/body/eval_jaxpr/while/body/eval_jaxpr/hqk,khs->qhs/dot_general | solution.py:50
  121.6 2.2 convolution_bitcast_fusion
  123.8 6.4 %copy.23 = f32[1,512,1152]{1,0,2:T(1,128)} copy(f32[1,512,1152]{2,1,0:T(8,128)} %convolution_bitcast_fusion) | data formatting | bytes 4718592 | tf_op jit(solution)/shard_map/fpe,ed->fpd/dot_general | solution.py:93
  132.2 65.7 %all-reduce.3.cloned.1.call-done = f32[1,512,1152]{1,0,2:T(1,128)} async-done(((f32[1,512,1152]{1,0,2:T(1,128)}), f32[1,512,1152]{1,0,2:T(1,128)}) %all-reduce.3.cloned.1.call-update) | async-done | bytes 2359312
  197.9 1.5 constant_dynamic-slice_fusion
  199.5 4.0 %collective-permute-start.4 = (bf16[1,512,288]{1,2,0:T(8,128)(2,1)S(1)}, bf16[1,512,288]{1,2,0:T(8,128)(2,1)S(1)}, u32[]{:S(2)}, u32[]{:S(2)}) collective-permute-start(bf16[1,512,288]{1,2,0:T(8,128)(2,1)S(1)} %fusion.31), channel_id=1, source_target_pairs={{0,4},{4,8},{8,12},{12,16},{16,20},{20,24},{24,28},{28,32},{32,36}... | collective-permute-start | bytes 884744 | tf_op jit(solution)/shard_map/ppermute | solution.py:28
  203.5 1.9 collective-permute-start.5
  205.5 5.2 %collective-permute-done.4 = bf16[1,512,288]{1,2,0:T(8,128)(2,1)S(1)} collective-permute-done((bf16[1,512,288]{1,2,0:T(8,128)(2,1)S(1)}, bf16[1,512,288]{1,2,0:T(8,128)(2,1)S(1)}, u32[]{:S(2)}, u32[]{:S(2)}) %collective-permute-start.4) | collective-permute-done | bytes 294944 | tf_op jit(solution)/shard_map/ppermute | solution.py:28
  210.7 9.4 %collective-permute-done.5 = bf16[1,512,288]{1,2,0:T(8,128)(2,1)S(1)} collective-permute-done((bf16[1,512,288]{1,2,0:T(8,128)(2,1)S(1)}, bf16[1,512,288]{1,2,0:T(8,128)(2,1)S(1)}, u32[]{:S(2)}, u32[]{:S(2)}) %collective-permute-start.5) | collective-permute-done | bytes 294944 | tf_op jit(solution)/shard_map/ppermute | solution.py:29
  220.2 0.9 fusion.23
  (31 shorter events, 4.0 us)
Async XLA Ops:
  6.5 30.2 %copy-start = (bf16[3,1152,288]{1,2,0:T(8,128)(2,1)S(1)}, bf16[3,1152,288]{1,2,0:T(8,128)(2,1)}, u32[]{:S(2)}) copy-start(bf16[3,1152,288]{1,2,0:T(8,128)(2,1)} %param.8) | copy-start | bytes 5971972
  6.5 26.9 %all-gather.2.cloned.1.call-start = ((), (), s32[]{:S(2)}) async-start(), calls=%async_computation | async-start | bytes 1474560 | tf_op jit(solution)/shard_map/all_gather | solution.py:60
  7.3 190.6 %all-reduce.3.cloned.1.call-start = ((), (), s32[]{:S(2)}) async-start(), calls=%async_computation.1 | async-start | bytes 4718592
  33.5 3.3 %copy-start.1 = (bf16[1,512,1152]{1,2,0:T(8,128)(2,1)S(1)}, bf16[1,512,1152]{1,2,0:T(8,128)(2,1)}, u32[]{:S(2)}) copy-start(bf16[1,512,1152]{1,2,0:T(8,128)(2,1)} %all-gather.2.cloned.1.call-done) | copy-start | bytes 3538948
  38.2 15.7 %collective-permute-start = (bf16[2,512,288]{1,2,0:T(8,128)(2,1)S(1)}, bf16[2,512,288]{1,2,0:T(8,128)(2,1)S(1)}, u32[]{:S(2)}, u32[]{:S(2)}) collective-permute-start(bf16[2,512,288]{1,2,0:T(8,128)(2,1)S(1)} %fusion.26), channel_id=1, source_target_pairs={{0,4},{4,0},{8,12},{12,8},{16,20},{20,16},{24,28},{28,24},{32,36},... | collective-permute-start | bytes 1769480 | tf_op jit(solution)/shard_map/ppermute | solution.py:18
  54.0 16.4 %collective-permute-start.1 = (bf16[2,512,288]{1,2,0:T(8,128)(2,1)S(1)}, bf16[2,512,288]{1,2,0:T(8,128)(2,1)S(1)}, u32[]{:S(2)}, u32[]{:S(2)}) collective-permute-start(bf16[2,512,288]{1,2,0:T(8,128)(2,1)S(1)} %fusion.47), channel_id=1, source_target_pairs={{0,8},{8,0},{4,12},{12,4},{16,24},{24,16},{20,28},{28,20},{32,40},... | collective-permute-start | bytes 1769480 | tf_op jit(solution)/shard_map/ppermute | solution.py:18
  70.6 14.0 %collective-permute-start.2 = (bf16[2,512,288]{1,2,0:T(8,128)(2,1)S(1)}, bf16[2,512,288]{1,2,0:T(8,128)(2,1)S(1)}, u32[]{:S(2)}, u32[]{:S(2)}) collective-permute-start(bf16[2,512,288]{1,2,0:T(8,128)(2,1)S(1)} %add.93), channel_id=1, source_target_pairs={{0,16},{16,0},{4,20},{20,4},{8,24},{24,8},{12,28},{28,12},{32,48},... | collective-permute-start | bytes 1769480 | tf_op jit(solution)/shard_map/ppermute | solution.py:18
  84.8 26.7 %collective-permute-start.3 = (bf16[2,512,288]{1,2,0:T(8,128)(2,1)S(1)}, bf16[2,512,288]{1,2,0:T(8,128)(2,1)S(1)}, u32[]{:S(2)}, u32[]{:S(2)}) collective-permute-start(bf16[2,512,288]{1,2,0:T(8,128)(2,1)S(1)} %add.94), channel_id=1, source_target_pairs={{0,32},{32,0},{4,36},{36,4},{8,40},{40,8},{12,44},{44,12},{16,48},... | collective-permute-start | bytes 1769480 | tf_op jit(solution)/shard_map/ppermute | solution.py:18
  116.7 4.9 %copy-start.3 = (bf16[288,1152]{1,0:T(8,128)(2,1)S(1)}, bf16[288,1152]{1,0:T(8,128)(2,1)}, u32[]{:S(2)}) copy-start(bf16[288,1152]{1,0:T(8,128)(2,1)} %param.9) | copy-start | bytes 1990660
  130.2 0.7 copy-start.5
  130.2 69.2 %copy-start.2 = (bf16[1,512,288]{1,2,0:T(8,128)(2,1)S(1)}, bf16[1,512,288]{1,2,0:T(8,128)(2,1)}, u32[]{:S(2)}) copy-start(bf16[1,512,288]{1,2,0:T(8,128)(2,1)} %param.6) | copy-start | bytes 884740
  130.2 75.2 %copy-start.4 = (f32[3,288]{1,0:T(4,128)S(1)}, f32[3,288]{1,0:T(4,128)}, u32[]{:S(2)}) copy-start(f32[3,288]{1,0:T(4,128)} %param.10) | copy-start | bytes 10372
  199.5 11.2 %collective-permute-start.4 = (bf16[1,512,288]{1,2,0:T(8,128)(2,1)S(1)}, bf16[1,512,288]{1,2,0:T(8,128)(2,1)S(1)}, u32[]{:S(2)}, u32[]{:S(2)}) collective-permute-start(bf16[1,512,288]{1,2,0:T(8,128)(2,1)S(1)} %fusion.31), channel_id=1, source_target_pairs={{0,4},{4,8},{8,12},{12,16},{16,20},{20,24},{24,28},{28,32},{32,36}... | collective-permute-start | bytes 884744 | tf_op jit(solution)/shard_map/ppermute | solution.py:28
  203.5 16.6 %collective-permute-start.5 = (bf16[1,512,288]{1,2,0:T(8,128)(2,1)S(1)}, bf16[1,512,288]{1,2,0:T(8,128)(2,1)S(1)}, u32[]{:S(2)}, u32[]{:S(2)}) collective-permute-start(bf16[1,512,288]{1,2,0:T(8,128)(2,1)S(1)} %fusion.31), channel_id=1, source_target_pairs={{4,0},{8,4},{12,8},{16,12},{20,16},{24,20},{28,24},{32,28},{36,32}... | collective-permute-start | bytes 884744 | tf_op jit(solution)/shard_map/ppermute | solution.py:29
Sparse Core Ops, SparseCore 0:
  9.1 24.2 all-gather.1
  130.4 67.4 all-reduce.2
where the time goes:
time: 228 us
  waiting for transfers between devices  171 us (75%)
  between operations  14.9 us (7%)
  matrix products  13.5 us (6%)
  starting transfers between devices  12.1 us (5%)
  local copies, waits for them, and re-layouts  10.6 us (5%)
  other arithmetic  5.89 us (3%)
    ppermute x4, waiting for transfers between devices, swapped(): return lax.ppermute(block, axis, route)  66.7 us
    unnamed x3, waiting for transfers between devices  66.4 us
    all_gather x1, waiting for transfers between devices, local(): gathered = lax.all_gather(frames, 'head', axis=2, tiled=True)  23.4 us
    ppermute x1, waiting for transfers between devices, extended(): after = lax.ppermute(leading, axis, down)  9.42 us
    dot_general x1, local copies, waits for them, and re-layouts, local(): jnp.einsum('fpe,ed->fpd', attended, w_out, preferred_element_type=jnp.flo...  6.39 us
    ppermute x4, starting transfers between devices, swapped(): return lax.ppermute(block, axis, route)  6.18 us
    ppermute x1, waiting for transfers between devices, extended(): before = lax.ppermute(last, axis, up)  5.21 us
    sub x1, matrix products, attend_block(): weights = jnp.exp(scores - row_max)  4.96 us
  transfers between devices with their start and end apart: 8, of which 8 were waited for; matrix products, arithmetic and copies ran while one was open for 1% of the time, Pallas kernels for 0%

commit v1 on v0

--- a/solution.py
+++ b/solution.py
@@ -57,7 +57,9 @@
     group_size = SEG // local_frames
     tm_pos = lax.axis_index("tm")
     head_pos = lax.axis_index("head")
-    gathered = lax.all_gather(frames, "head", axis=2, tiled=True)
+    gathered = jnp.concatenate(
+        lax.all_to_all(jnp.stack([frames] * lax.axis_size("head")), "head", 0, 0), axis=2
+    )
     normed = modulate(gathered, modulation)
     projections = jnp.einsum(
         "fpd,cde->cfpe", normed, w_qkv, preferred_element_type=jnp.float32

time: 228 us -> 217 us (0.952)
  waiting for transfers between devices: 171 us -> 159 us
  other arithmetic: 5.89 us -> 3.09 us
  starting transfers between devices: 12.1 us -> 14.5 us
    all_gather x1 -> x0, waiting for transfers between devices: 23.4 us -> none  [local(): gathered = lax.all_gather(frames, 'head', axis=2, tiled=True)]
    all_to_all x0 -> x1, waiting for transfers between devices: none -> 14.4 us  [local(): lax.all_to_all(jnp.stack([frames] * lax.axis_size('head')), 'head', 0, 0)]
    all_to_all x0 -> x1, starting transfers between devices: none -> 3.53 us  [local(): lax.all_to_all(jnp.stack([frames] * lax.axis_size('head')), 'head', 0, 0)]
    ppermute x4, waiting for transfers between devices: 66.7 us -> 64.2 us  [swapped(): return lax.ppermute(block, axis, route)]
    unnamed x3 -> x2, waiting for transfers between devices: 66.4 us -> 65.5 us
where the time goes in v1:
time: 217 us
  waiting for transfers between devices  159 us (73%)
  between operations  14.9 us (7%)
  starting transfers between devices  14.5 us (7%)
  matrix products  13.4 us (6%)
  local copies, waits for them, and re-layouts  12.1 us (6%)
  other arithmetic  3.09 us (1%)
    unnamed x2, waiting for transfers between devices  65.5 us
    ppermute x4, waiting for transfers between devices, swapped(): return lax.ppermute(block, axis, route)  64.2 us
    all_to_all x1, waiting for transfers between devices, local(): lax.all_to_all(jnp.stack([frames] * lax.axis_size('head')), 'head', 0, 0)  14.4 us
    ppermute x1, waiting for transfers between devices, extended(): after = lax.ppermute(leading, axis, down)  9.42 us
    dot_general x1, local copies, waits for them, and re-layouts, local(): jnp.einsum('fpe,ed->fpd', attended, w_out, preferred_element_type=jnp.flo...  6.39 us
    ppermute x1, waiting for transfers between devices, extended(): before = lax.ppermute(last, axis, up)  5.21 us
    ppermute x4, starting transfers between devices, swapped(): return lax.ppermute(block, axis, route)  5.04 us
    sub x1, matrix products, attend_block(): weights = jnp.exp(scores - row_max)  4.96 us
  transfers between devices with their start and end apart: 8, of which 8 were waited for; matrix products, arithmetic and copies ran while one was open for 1% of the time, Pallas kernels for 0%

profile of v1, /device:TPU:230, one launch (start us, length us, event | category | flops | bytes accessed | tf_op | source)
XLA Modules:
  0.0 216.8 jit_solution(958786207511863751)
XLA Ops:
  6.5 2.2 %stack.2 = bf16[4,1,512,288]{2,3,1,0:T(8,128)(2,1)} broadcast(bf16[512,288]{0,1:T(8,128)(2,1)} %bitcast.54), dimensions={2,3} | broadcast | bytes 1474560 | tf_op jit(solution)/shard_map/stack | solution.py:61
  8.7 3.5 %all-to-all-start = ((bf16[4,1,512,288]{2,3,1,0:T(8,128)(2,1)}), bf16[4,1,512,288]{2,3,1,0:T(8,128)(2,1)S(1)}, u32[]{:S(2)}, u32[]{:S(2)}) async-start(bf16[4,1,512,288]{2,3,1,0:T(8,128)(2,1)} %stack.2), calls=%async_computation | async-start | bytes 2359296 | tf_op jit(solution)/shard_map/all_to_all | solution.py:61
  13.7 14.4 %all-to-all-done = bf16[4,1,512,288]{2,3,1,0:T(8,128)(2,1)S(1)} async-done(((bf16[4,1,512,288]{2,3,1,0:T(8,128)(2,1)}), bf16[4,1,512,288]{2,3,1,0:T(8,128)(2,1)S(1)}, u32[]{:S(2)}, u32[]{:S(2)}) %all-to-all-start) | async-done | bytes 1179680 | tf_op jit(solution)/shard_map/all_to_all | solution.py:61
  29.4 1.3 fusion.12
  30.8 0.9 collective-permute-start
  31.7 13.9 %collective-permute-done = bf16[2,512,288]{1,2,0:T(8,128)(2,1)S(1)} collective-permute-done((bf16[2,512,288]{1,2,0:T(8,128)(2,1)S(1)}, bf16[2,512,288]{1,2,0:T(8,128)(2,1)S(1)}, u32[]{:S(2)}, u32[]{:S(2)}) %collective-permute-start) | collective-permute-done | bytes 589856 | tf_op jit(solution)/shard_map/ppermute | solution.py:18
  45.7 1.5 collective-permute-start.1
  47.2 14.0 %collective-permute-done.1 = bf16[2,512,288]{1,2,0:T(8,128)(2,1)S(1)} collective-permute-done((bf16[2,512,288]{1,2,0:T(8,128)(2,1)S(1)}, bf16[2,512,288]{1,2,0:T(8,128)(2,1)S(1)}, u32[]{:S(2)}, u32[]{:S(2)}) %collective-permute-start.1) | collective-permute-done | bytes 589856 | tf_op jit(solution)/shard_map/ppermute | solution.py:18
  61.4 1.1 collective-permute-start.2
  62.5 12.1 %collective-permute-done.2 = bf16[2,512,288]{1,2,0:T(8,128)(2,1)S(1)} collective-permute-done((bf16[2,512,288]{1,2,0:T(8,128)(2,1)S(1)}, bf16[2,512,288]{1,2,0:T(8,128)(2,1)S(1)}, u32[]{:S(2)}, u32[]{:S(2)}) %collective-permute-start.2) | collective-permute-done | bytes 589856 | tf_op jit(solution)/shard_map/ppermute | solution.py:18
  74.7 1.5 collective-permute-start.3
  76.3 24.2 %collective-permute-done.3 = bf16[2,512,288]{1,2,0:T(8,128)(2,1)S(1)} collective-permute-done((bf16[2,512,288]{1,2,0:T(8,128)(2,1)S(1)}, bf16[2,512,288]{1,2,0:T(8,128)(2,1)S(1)}, u32[]{:S(2)}, u32[]{:S(2)}) %collective-permute-start.3) | collective-permute-done | bytes 589856 | tf_op jit(solution)/shard_map/ppermute | solution.py:18
  100.7 5.0 %fusion.37 = (f32[4,512]{1,0:T(4,128)S(1)}, f32[4,512,1024]{2,1,0:T(8,128)}) fusion(bf16[512,4,72]{0,2,1:T(8,128)(2,1)S(1)} %bitcast.58, bf16[512,4,72]{0,2,1:T(8,128)(2,1)S(1)} %bitcast.60, bf16[512,4,72]{0,2,1:T(8,128)(2,1)S(1)} %bitcast.57), kind=kOutput, calls=%fused_computation.55 | convolution fusion | flops 309462016 | bytes 9281536 | tf_op jit(solution)/shard_map/while/body/eval_jaxpr/while/body/eval_jaxpr/sub | solution.py:48
  105.7 4.9 %fusion.13 = bf16[4,72,512]{2,1,0:T(8,128)(2,1)S(1)} fusion(f32[4,512,1024]{2,1,0:T(8,128)} %get-tuple-element.58, f32[4,512]{1,0:T(4,128)S(1)} %get-tuple-element.57, bf16[512,4,72]{0,2,1:T(8,128)(2,1)S(1)} %bitcast.59, bf16[512,4,72]{0,2,1:T(8,128)(2,1)S(1)} %bitcast.56), kind=kOutput, calls=%fused_computation.18 | convolution fusion | flops 307511296 | bytes 9281536 | tf_op jit(solution)/shard_map/while/body/eval_jaxpr/while/body/eval_jaxpr/hqk,khs->qhs/dot_general | solution.py:50
  110.6 2.3 %convolution_bitcast_fusion = f32[1,512,1152]{2,1,0:T(8,128)} fusion(bf16[512,288]{0,1:T(8,128)(2,1)S(1)} %bitcast.55, bf16[288,1152]{1,0:T(8,128)(2,1)S(1)} %copy-done.2), kind=kOutput, calls=%fused_computation.7 | convolution fusion | flops 339738624 | bytes 3317760 | tf_op jit(solution)/shard_map/fpe,ed->fpd/dot_general | solution.py:95
  112.8 6.4 %copy.29 = f32[1,512,1152]{1,0,2:T(1,128)} copy(f32[1,512,1152]{2,1,0:T(8,128)} %convolution_bitcast_fusion) | data formatting | bytes 4718592 | tf_op jit(solution)/shard_map/fpe,ed->fpd/dot_general | solution.py:95
  119.3 0.6 copy-done.6
  121.2 65.4 %all-reduce.3.cloned.1.call-done = f32[1,512,1152]{1,0,2:T(1,128)} async-done(((f32[1,512,1152]{1,0,2:T(1,128)}), f32[1,512,1152]{1,0,2:T(1,128)}) %all-reduce.3.cloned.1.call-update) | async-done | bytes 2359312
  186.7 1.5 constant_dynamic-slice_fusion
  188.3 4.0 %collective-permute-start.4 = (bf16[1,512,288]{1,2,0:T(8,128)(2,1)S(1)}, bf16[1,512,288]{1,2,0:T(8,128)(2,1)S(1)}, u32[]{:S(2)}, u32[]{:S(2)}) collective-permute-start(bf16[1,512,288]{1,2,0:T(8,128)(2,1)S(1)} %fusion.27), channel_id=1, source_target_pairs={{0,4},{4,8},{8,12},{12,16},{16,20},{20,24},{24,28},{28,32},{32,36}... | collective-permute-start | bytes 884744 | tf_op jit(solution)/shard_map/ppermute | solution.py:28
  192.3 1.9 collective-permute-start.5
  194.3 5.2 %collective-permute-done.4 = bf16[1,512,288]{1,2,0:T(8,128)(2,1)S(1)} collective-permute-done((bf16[1,512,288]{1,2,0:T(8,128)(2,1)S(1)}, bf16[1,512,288]{1,2,0:T(8,128)(2,1)S(1)}, u32[]{:S(2)}, u32[]{:S(2)}) %collective-permute-start.4) | collective-permute-done | bytes 294944 | tf_op jit(solution)/shard_map/ppermute | solution.py:28
  199.5 9.4 %collective-permute-done.5 = bf16[1,512,288]{1,2,0:T(8,128)(2,1)S(1)} collective-permute-done((bf16[1,512,288]{1,2,0:T(8,128)(2,1)S(1)}, bf16[1,512,288]{1,2,0:T(8,128)(2,1)S(1)}, u32[]{:S(2)}, u32[]{:S(2)}) %collective-permute-start.5) | collective-permute-done | bytes 294944 | tf_op jit(solution)/shard_map/ppermute | solution.py:29
  209.0 0.9 fusion.19
  (35 shorter events, 3.6 us)
Async XLA Ops:
  6.5 22.9 %copy-start = (bf16[3,1152,288]{1,2,0:T(8,128)(2,1)S(1)}, bf16[3,1152,288]{1,2,0:T(8,128)(2,1)}, u32[]{:S(2)}) copy-start(bf16[3,1152,288]{1,2,0:T(8,128)(2,1)} %param.8) | copy-start | bytes 5971972
  6.5 5.8 %copy-start.5 = (s32[4]{0:T(128)S(1)}, s32[4]{0:T(128)}, u32[]{:S(2)}) copy-start(s32[4]{0:T(128)} %param.11) | copy-start | bytes 52
  6.5 7.1 %copy-start.3 = (f32[3,1152]{1,0:T(4,128)S(1)}, f32[3,1152]{1,0:T(4,128)}, u32[]{:S(2)}) copy-start(f32[3,1152]{1,0:T(4,128)} %param.7) | copy-start | bytes 41476
  8.7 19.3 %all-to-all-start = ((bf16[4,1,512,288]{2,3,1,0:T(8,128)(2,1)}), bf16[4,1,512,288]{2,3,1,0:T(8,128)(2,1)S(1)}, u32[]{:S(2)}, u32[]{:S(2)}) async-start(bf16[4,1,512,288]{2,3,1,0:T(8,128)(2,1)} %stack.2), calls=%async_computation | async-start | bytes 2359296 | tf_op jit(solution)/shard_map/all_to_all | solution.py:61
  12.3 174.4 %all-reduce.3.cloned.1.call-start = ((), (), s32[]{:S(2)}) async-start(), calls=%async_computation.1 | async-start | bytes 4718592
  30.8 14.9 %collective-permute-start = (bf16[2,512,288]{1,2,0:T(8,128)(2,1)S(1)}, bf16[2,512,288]{1,2,0:T(8,128)(2,1)S(1)}, u32[]{:S(2)}, u32[]{:S(2)}) collective-permute-start(bf16[2,512,288]{1,2,0:T(8,128)(2,1)S(1)} %fusion.22), channel_id=1, source_target_pairs={{0,4},{4,0},{8,12},{12,8},{16,20},{20,16},{24,28},{28,24},{32,36},... | collective-permute-start | bytes 1769480 | tf_op jit(solution)/shard_map/ppermute | solution.py:18
  45.7 15.5 %collective-permute-start.1 = (bf16[2,512,288]{1,2,0:T(8,128)(2,1)S(1)}, bf16[2,512,288]{1,2,0:T(8,128)(2,1)S(1)}, u32[]{:S(2)}, u32[]{:S(2)}) collective-permute-start(bf16[2,512,288]{1,2,0:T(8,128)(2,1)S(1)} %fusion.43), channel_id=1, source_target_pairs={{0,8},{8,0},{4,12},{12,4},{16,24},{24,16},{20,28},{28,20},{32,40},... | collective-permute-start | bytes 1769480 | tf_op jit(solution)/shard_map/ppermute | solution.py:18
  61.4 13.1 %collective-permute-start.2 = (bf16[2,512,288]{1,2,0:T(8,128)(2,1)S(1)}, bf16[2,512,288]{1,2,0:T(8,128)(2,1)S(1)}, u32[]{:S(2)}, u32[]{:S(2)}) collective-permute-start(bf16[2,512,288]{1,2,0:T(8,128)(2,1)S(1)} %add.93), channel_id=1, source_target_pairs={{0,16},{16,0},{4,20},{20,4},{8,24},{24,8},{12,28},{28,12},{32,48},... | collective-permute-start | bytes 1769480 | tf_op jit(solution)/shard_map/ppermute | solution.py:18
  74.7 25.8 %collective-permute-start.3 = (bf16[2,512,288]{1,2,0:T(8,128)(2,1)S(1)}, bf16[2,512,288]{1,2,0:T(8,128)(2,1)S(1)}, u32[]{:S(2)}, u32[]{:S(2)}) collective-permute-start(bf16[2,512,288]{1,2,0:T(8,128)(2,1)S(1)} %add.94), channel_id=1, source_target_pairs={{0,32},{32,0},{4,36},{36,4},{8,40},{40,8},{12,44},{44,12},{16,48},... | collective-permute-start | bytes 1769480 | tf_op jit(solution)/shard_map/ppermute | solution.py:18
  105.7 4.9 %copy-start.2 = (bf16[288,1152]{1,0:T(8,128)(2,1)S(1)}, bf16[288,1152]{1,0:T(8,128)(2,1)}, u32[]{:S(2)}) copy-start(bf16[288,1152]{1,0:T(8,128)(2,1)} %param.9) | copy-start | bytes 1990660
  119.2 0.7 copy-start.6
  119.2 68.9 %copy-start.1 = (bf16[1,512,288]{1,2,0:T(8,128)(2,1)S(1)}, bf16[1,512,288]{1,2,0:T(8,128)(2,1)}, u32[]{:S(2)}) copy-start(bf16[1,512,288]{1,2,0:T(8,128)(2,1)} %param.6) | copy-start | bytes 884740
  119.2 75.0 %copy-start.4 = (f32[3,288]{1,0:T(4,128)S(1)}, f32[3,288]{1,0:T(4,128)}, u32[]{:S(2)}) copy-start(f32[3,288]{1,0:T(4,128)} %param.10) | copy-start | bytes 10372
  188.3 11.2 %collective-permute-start.4 = (bf16[1,512,288]{1,2,0:T(8,128)(2,1)S(1)}, bf16[1,512,288]{1,2,0:T(8,128)(2,1)S(1)}, u32[]{:S(2)}, u32[]{:S(2)}) collective-permute-start(bf16[1,512,288]{1,2,0:T(8,128)(2,1)S(1)} %fusion.27), channel_id=1, source_target_pairs={{0,4},{4,8},{8,12},{12,16},{16,20},{20,24},{24,28},{28,32},{32,36}... | collective-permute-start | bytes 884744 | tf_op jit(solution)/shard_map/ppermute | solution.py:28
  192.3 16.6 %collective-permute-start.5 = (bf16[1,512,288]{1,2,0:T(8,128)(2,1)S(1)}, bf16[1,512,288]{1,2,0:T(8,128)(2,1)S(1)}, u32[]{:S(2)}, u32[]{:S(2)}) collective-permute-start(bf16[1,512,288]{1,2,0:T(8,128)(2,1)S(1)} %fusion.27), channel_id=1, source_target_pairs={{4,0},{8,4},{12,8},{16,12},{20,16},{24,20},{28,24},{32,28},{36,32}... | collective-permute-start | bytes 884744 | tf_op jit(solution)/shard_map/ppermute | solution.py:29
Sparse Core Ops, SparseCore 0:
  119.4 67.2 all-reduce.2
